TPU v7x, 512 devices: a whole 4x8x8 slice. The times are simulated.
512 devices in a mesh: span: 16 (over z_hi, x), wall: 16 (over y, core), stream: 2 (over z_lo).
Axes of the slice: x: 4, y: 8, z: 8 (z_hi: 4, z_lo: 2; z = z_hi * 2 + z_lo), core: 2. Of those that a mesh axis runs over, the one named last changes fastest.
Arguments:
- fields: float32 [4, 16, 256, 2048], P(None, 'stream', 'wall', 'span'), may hold values from -67.5 to 67.5, as said below
Outputs:
- clark_model: float32 [3, 16, 256, 2048], P(None, 'stream', 'wall', 'span')
- similar_model: float32 [3, 16, 256, 2048], P(None, 'stream', 'wall', 'span')
- clark_corr: float32 [3, 256], P(None, 'wall')
- similar_corr: float32 [3, 256], P(None, 'wall')
Inputs may be any that keep to these rules, and one draw needn't show every extreme that they name: The fields are rough from cell to cell.
All inputs are finite; a program needn't handle non-finite values.
Results may differ from a plain program's by a relative error of at most 0.00024.
Values sent between devices are 32-bit elements; how exact they have to be, the bound alone decides.
A program may use at most 64 MiB of HBM per device.

v0:
```python
import math
import jax
import jax.numpy as jnp
from jax import lax
from jax.sharding import PartitionSpec as P

raw_taps = [math.exp(-((k - 8) ** 2) / 18.0) for k in range(17)]
filter_taps = [value / sum(raw_taps) for value in raw_taps]
clark_coef = 9.0
small_eps = 1e-06


def with_halo(cells, sides, width, closed):
    for axis, dim in sides:
        count = lax.axis_size(axis)
        ends = count if closed else count - 1
        head = lax.slice_in_dim(cells, 0, width, axis=dim)
        tail = lax.slice_in_dim(cells, cells.shape[dim] - width, cells.shape[dim], axis=dim)
        cells = jnp.concatenate(
            [
                lax.ppermute(tail, axis, [(i, (i + 1) % count) for i in range(ends)]),
                cells,
                lax.ppermute(head, axis, [((i + 1) % count, i) for i in range(ends)]),
            ],
            axis=dim,
        )
    return cells


def band_matrix(length):
    offset = (
        jnp.arange(length + 16, dtype=jnp.int32)[:, None]
        - jnp.arange(length, dtype=jnp.int32)[None, :]
    )
    matrix = jnp.zeros((length + 16, length), jnp.float32)
    for k in range(17):
        matrix = matrix + jnp.where(offset == k, filter_taps[k], 0.0).astype(jnp.float32)
    return matrix


def smooth(padded, direction, length):
    matrix = band_matrix(length)
    if direction == 3:
        return jnp.einsum("fswz,zk->fswk", padded, matrix, precision=lax.Precision.HIGHEST)
    if direction == 2:
        return jnp.einsum("fswz,wk->fskz", padded, matrix, precision=lax.Precision.HIGHEST)
    return jnp.einsum("fswz,sk->fkwz", padded, matrix, precision=lax.Precision.HIGHEST)


def with_products(quad):
    return jnp.concatenate([quad, quad[:3] * quad[3:4]], axis=0)


def filter_all(quad):
    stream_len, wall_len, span_len = (quad.shape[1], quad.shape[2], quad.shape[3])
    payload = with_products(quad)
    spanned = with_halo(payload, (("span", 3),), 8, True)
    extended = with_halo(spanned, (("wall", 2), ("stream", 1)), 8, False)
    kept = extended[:4]
    result = smooth(extended, 3, span_len)
    result = smooth(result, 2, wall_len)
    return (smooth(result, 1, stream_len), kept)


def clark_flux(means):
    padded = with_halo(means, (("span", 3),), 1, True)
    along_span = (padded[..., 2:] - padded[..., :-2]) * 0.5
    plane = with_halo(means, (("wall", 2), ("stream", 1)), 1, False)
    along_wall = (plane[:, 1:-1, 2:, :] - plane[:, 1:-1, :-2, :]) * 0.5
    along_stream = (plane[:, 2:, 1:-1, :] - plane[:, :-2, 1:-1, :]) * 0.5
    total = along_span[:3] * along_span[3:4] + along_wall[:3] * along_wall[3:4]
    total = total + along_stream[:3] * along_stream[3:4]
    return clark_coef * total


def shards(fields):
    first, unused_rim = filter_all(fields)
    means = first[:4]
    exact = first[4:] - means[:3] * means[3:4]
    second, mean_rim = filter_all(means)
    similar = second[4:] - second[:3] * second[3:4]
    clark = clark_flux(means)
    sums = (
        jnp.sum(exact * clark, axis=(1, 3)),
        jnp.sum(exact * similar, axis=(1, 3)),
        jnp.sum(exact * exact, axis=(1, 3)),
        jnp.sum(clark * clark, axis=(1, 3)),
        jnp.sum(similar * similar, axis=(1, 3)),
    )
    cross_c, cross_s, power_e, power_c, power_s = lax.psum(
        (sums[0], sums[1], sums[2], sums[3], sums[4]), ("span", "stream")
    )
    plane_cells = float(
        fields.shape[1] * fields.shape[3] * lax.axis_size("stream") * lax.axis_size("span")
    )
    cross_c = cross_c / plane_cells
    cross_s = cross_s / plane_cells
    power_e = power_e / plane_cells
    power_c = power_c / plane_cells
    power_s = power_s / plane_cells
    clark_corr = cross_c / jnp.sqrt((power_e + small_eps) * (power_c + small_eps))
    similar_corr = cross_s / jnp.sqrt((power_e + small_eps) * (power_s + small_eps))
    clark_model = clark / jnp.sqrt(power_c + small_eps)[:, None, :, None]
    similar_model = similar / jnp.sqrt(power_s + small_eps)[:, None, :, None]
    return (clark_model, similar_model, clark_corr, similar_corr)


def solution(mesh):
    return jax.shard_map(
        shards,
        mesh=mesh,
        in_specs=(P(None, "stream", "wall", "span"),),
        out_specs=(
            P(None, "stream", "wall", "span"),
            P(None, "stream", "wall", "span"),
            P(None, "wall"),
            P(None, "wall"),
        ),
        check_vma=False,
    )
```

profile of v0, /device:TPU:16, one launch (start us, length us, event | category | flops | bytes accessed | tf_op | source)
XLA Modules:
  0.0 371.7 jit_solution(2666519787292298506)
XLA Ops:
  3.7 13.1 %collective-permute-start.1 = (f32[7,8,16,8]{3,2,1,0:T(8,128)S(1)}, f32[7,8,16,8]{3,2,1,0:T(8,128)S(1)}, u32[]{:S(2)}, u32[]{:S(2)}) collective-permute-start(f32[7,8,16,8]{3,2,1,0:T(8,128)S(1)} %get-tuple-element.31), channel_id=1, source_target_pairs={{32,0},{64,32},{96,64},{128,96},{160,128},{192,160},{224,192},{256... | collective-permute-start | bytes 86024 | tf_op jit(solution)/shard_map/ppermute | solution.py:23
  18.8 17.7 %collective-permute-done.1 = f32[7,8,16,8]{3,2,1,0:T(8,128)S(1)} collective-permute-done((f32[7,8,16,8]{3,2,1,0:T(8,128)S(1)}, f32[7,8,16,8]{3,2,1,0:T(8,128)S(1)}, u32[]{:S(2)}, u32[]{:S(2)}) %collective-permute-start.1) | collective-permute-done | bytes 28704 | tf_op jit(solution)/shard_map/ppermute | solution.py:23
  36.4 8.3 %collective-permute-done = f32[7,8,16,8]{3,2,1,0:T(8,128)S(1)} collective-permute-done((f32[7,8,16,8]{3,2,1,0:T(8,128)S(1)}, f32[7,8,16,8]{3,2,1,0:T(8,128)S(1)}, u32[]{:S(2)}, u32[]{:S(2)}) %collective-permute-start) | collective-permute-done | bytes 28704 | tf_op jit(solution)/shard_map/ppermute | solution.py:21
  48.2 2.4 collective-permute-start.2
  50.6 3.6 collective-permute-done.3
  54.2 3.8 %collective-permute-done.2 = f32[7,8,8,144]{3,2,1,0:T(8,128)S(1)} collective-permute-done((f32[7,8,8,144]{3,2,1,0:T(8,128)S(1)}, f32[7,8,8,144]{3,2,1,0:T(8,128)S(1)}, u32[]{:S(2)}, u32[]{:S(2)}) %collective-permute-start.2) | collective-permute-done | bytes 258080 | tf_op jit(solution)/shard_map/ppermute | solution.py:21
  59.8 4.8 %collective-permute-start.4 = (f32[7,8,32,144]{3,2,1,0:T(8,128)S(1)}, f32[7,8,32,144]{3,2,1,0:T(8,128)S(1)}, u32[]{:S(2)}, u32[]{:S(2)}) collective-permute-start(f32[7,8,32,144]{3,2,1,0:T(8,128)S(1)} %pad_maximum_fusion.1), channel_id=1, source_target_pairs={{0,1},{2,3},{4,5},{6,7},{8,9},{10,11},{12,13},{14,15},{16,17},{18,... | collective-permute-start | bytes 3096584 | tf_op jit(solution)/shard_map/ppermute | solution.py:21
  64.5 36.9 %collective-permute-done.5 = f32[7,8,32,144]{3,2,1,0:T(8,128)S(1)} collective-permute-done((f32[7,8,32,144]{3,2,1,0:T(8,128)S(1)}, f32[7,8,32,144]{3,2,1,0:T(8,128)S(1)}, u32[]{:S(2)}, u32[]{:S(2)}) %collective-permute-start.5) | collective-permute-done | bytes 1032224 | tf_op jit(solution)/shard_map/ppermute | solution.py:23
  102.8 4.7 %fusion = f32[7,24,32,128]{3,2,1,0:T(8,128)S(1)} fusion(f32[7,8,32,144]{3,2,1,0:T(8,128)S(1)} %collective-permute-done.5, f32[7,8,8,144]{3,2,1,0:T(8,128)S(1)} %collective-permute-done.3, f32[7,8,16,8]{3,2,1,0:T(8,128)S(1)} %collective-permute-done.1, f32[3,8,16,128]{3,2,1,0:T(8,128)S(1)} %slice_multiply_fusion.5, f32[4,8,16,128]{3,2,1,0:T(8,128)S(1)} %copy-done, ...), kind=kOutput, calls=%fused_computation | convolution fusion | flops 1195444224 | bytes 5849088 | tf_op jit(solution)/shard_map/fswz,zk->fswk/dot_general | solution.py:44
  112.4 3.9 %collective-permute-start.12 = (f32[7,8,16,8]{3,1,2,0:T(8,128)S(1)}, f32[7,8,16,8]{3,1,2,0:T(8,128)S(1)}, u32[]{:S(2)}, u32[]{:S(2)}) collective-permute-start(f32[7,8,16,8]{3,1,2,0:T(8,128)S(1)} %get-tuple-element.28), channel_id=1, source_target_pairs={{0,32},{32,64},{64,96},{96,128},{128,160},{160,192},{192,224},{224... | collective-permute-start | bytes 86024 | tf_op jit(solution)/shard_map/ppermute | solution.py:21
  116.3 14.1 %collective-permute-done.13 = f32[7,8,16,8]{3,1,2,0:T(8,128)S(1)} collective-permute-done((f32[7,8,16,8]{3,1,2,0:T(8,128)S(1)}, f32[7,8,16,8]{3,1,2,0:T(8,128)S(1)}, u32[]{:S(2)}, u32[]{:S(2)}) %collective-permute-start.13) | collective-permute-done | bytes 28704 | tf_op jit(solution)/shard_map/ppermute | solution.py:23
  130.4 8.3 %collective-permute-done.12 = f32[7,8,16,8]{3,1,2,0:T(8,128)S(1)} collective-permute-done((f32[7,8,16,8]{3,1,2,0:T(8,128)S(1)}, f32[7,8,16,8]{3,1,2,0:T(8,128)S(1)}, u32[]{:S(2)}, u32[]{:S(2)}) %collective-permute-start.12) | collective-permute-done | bytes 28704 | tf_op jit(solution)/shard_map/ppermute | solution.py:21
  141.2 2.4 collective-permute-start.14
  143.6 3.6 collective-permute-done.15
  147.2 3.8 %collective-permute-done.14 = f32[7,8,8,144]{3,1,2,0:T(8,128)S(1)} collective-permute-done((f32[7,8,8,144]{3,1,2,0:T(8,128)S(1)}, f32[7,8,8,144]{3,1,2,0:T(8,128)S(1)}, u32[]{:S(2)}, u32[]{:S(2)}) %collective-permute-start.14) | collective-permute-done | bytes 258080 | tf_op jit(solution)/shard_map/ppermute | solution.py:21
  152.7 4.8 %collective-permute-start.16 = (f32[7,8,32,144]{3,1,2,0:T(8,128)S(1)}, f32[7,8,32,144]{3,1,2,0:T(8,128)S(1)}, u32[]{:S(2)}, u32[]{:S(2)}) collective-permute-start(f32[7,8,32,144]{3,1,2,0:T(8,128)S(1)} %pad_maximum_fusion.2), channel_id=1, source_target_pairs={{0,1},{2,3},{4,5},{6,7},{8,9},{10,11},{12,13},{14,15},{16,17},{18,... | collective-permute-start | bytes 3096584 | tf_op jit(solution)/shard_map/ppermute | solution.py:21
  157.5 3.3 collective-permute-start.9
  160.8 2.5 collective-permute-start.8
  163.3 3.1 collective-permute-done.8
  171.2 38.2 %collective-permute-done.7 = f32[4,8,16,1]{3,1,2,0:T(8,128)S(1)} collective-permute-done((f32[4,8,16,1]{3,1,2,0:T(8,128)S(1)}, f32[4,8,16,1]{3,1,2,0:T(8,128)S(1)}, u32[]{:S(2)}, u32[]{:S(2)}) %collective-permute-start.7) | collective-permute-done | bytes 2080 | tf_op jit(solution)/shard_map/ppermute | solution.py:21
  211.2 8.4 %collective-permute-done.6 = f32[4,8,16,1]{3,1,2,0:T(8,128)S(1)} collective-permute-done((f32[4,8,16,1]{3,1,2,0:T(8,128)S(1)}, f32[4,8,16,1]{3,1,2,0:T(8,128)S(1)}, u32[]{:S(2)}, u32[]{:S(2)}) %collective-permute-start.6) | collective-permute-done | bytes 2080 | tf_op jit(solution)/shard_map/ppermute | solution.py:23
  220.1 2.6 pad_maximum_fusion
  222.7 5.8 %fusion.16 = f32[7,24,32,128]{3,2,1,0:T(8,128)S(1)} fusion(f32[7,24,32,144]{3,1,2,0:T(8,128)S(1)} %pad_maximum_fusion), kind=kOutput, calls=%fused_computation.17 | convolution fusion | flops 1190025216 | bytes 5849088 | tf_op jit(solution)/shard_map/fswz,zk->fswk/dot_general | solution.py:44
  231.8 137.7 %all-reduce = (f32[3,16]{1,0:T(4,128)S(1)}, f32[3,16]{1,0:T(4,128)S(1)}, f32[3,16]{1,0:T(4,128)S(1)}, f32[3,16]{1,0:T(4,128)S(1)}, f32[3,16]{1,0:T(4,128)S(1)}) all-reduce(f32[3,16]{1,0:T(4,128)S(1)} %get-tuple-element.11, f32[3,16]{1,0:T(4,128)S(1)} %get-tuple-element.12, ...), channel_id=1, replica_groups=mesh['span'=16,'wall'=16,'stream'=2] {'span','stream'}, use_global_device_ids=true, to_apply=%region_1.2 | all-reduce | flops 240 | bytes 1920 | tf_op jit(solution)/shard_map/psum | solution.py:90
  (48 shorter events, 32.9 us)
Async XLA Ops:
  2.4 55.6 %copy-start = (f32[4,8,16,128]{3,2,1,0:T(8,128)S(1)}, f32[4,8,16,128]{3,2,1,0:T(8,128)}, u32[]{:S(2)}) copy-start(f32[4,8,16,128]{3,2,1,0:T(8,128)} %param.1) | copy-start | bytes 786436
  3.7 32.7 %collective-permute-start.1 = (f32[7,8,16,8]{3,2,1,0:T(8,128)S(1)}, f32[7,8,16,8]{3,2,1,0:T(8,128)S(1)}, u32[]{:S(2)}, u32[]{:S(2)}) collective-permute-start(f32[7,8,16,8]{3,2,1,0:T(8,128)S(1)} %get-tuple-element.31), channel_id=1, source_target_pairs={{32,0},{64,32},{96,64},{128,96},{160,128},{192,160},{224,192},{256... | collective-permute-start | bytes 86024 | tf_op jit(solution)/shard_map/ppermute | solution.py:23
  16.9 27.9 %collective-permute-start = (f32[7,8,16,8]{3,2,1,0:T(8,128)S(1)}, f32[7,8,16,8]{3,2,1,0:T(8,128)S(1)}, u32[]{:S(2)}, u32[]{:S(2)}) collective-permute-start(f32[7,8,16,8]{3,2,1,0:T(8,128)S(1)} %get-tuple-element.30), channel_id=1, source_target_pairs={{0,32},{32,64},{64,96},{96,128},{128,160},{160,192},{192,224},{224... | collective-permute-start | bytes 86024 | tf_op jit(solution)/shard_map/ppermute | solution.py:21
  46.3 7.9 %collective-permute-start.3 = (f32[7,8,8,144]{3,2,1,0:T(8,128)S(1)}, f32[7,8,8,144]{3,2,1,0:T(8,128)S(1)}, u32[]{:S(2)}, u32[]{:S(2)}) collective-permute-start(f32[7,8,8,144]{3,2,1,0:T(8,128)S(1)} %get-tuple-element.23), channel_id=1, source_target_pairs={{2,0},{4,2},{6,4},{8,6},{10,8},{12,10},{14,12},{16,14},{18,16},{20... | collective-permute-start | bytes 774152 | tf_op jit(solution)/shard_map/ppermute | solution.py:23
  48.2 9.8 %collective-permute-start.2 = (f32[7,8,8,144]{3,2,1,0:T(8,128)S(1)}, f32[7,8,8,144]{3,2,1,0:T(8,128)S(1)}, u32[]{:S(2)}, u32[]{:S(2)}) collective-permute-start(f32[7,8,8,144]{3,2,1,0:T(8,128)S(1)} %get-tuple-element.22), channel_id=1, source_target_pairs={{0,2},{2,4},{4,6},{6,8},{8,10},{10,12},{12,14},{14,16},{16,18},{18... | collective-permute-start | bytes 774152 | tf_op jit(solution)/shard_map/ppermute | solution.py:21
  58.5 43.0 %collective-permute-start.5 = (f32[7,8,32,144]{3,2,1,0:T(8,128)S(1)}, f32[7,8,32,144]{3,2,1,0:T(8,128)S(1)}, u32[]{:S(2)}, u32[]{:S(2)}) collective-permute-start(f32[7,8,32,144]{3,2,1,0:T(8,128)S(1)} %pad_maximum_fusion.1), channel_id=1, source_target_pairs={{1,0},{3,2},{5,4},{7,6},{9,8},{11,10},{13,12},{15,14},{17,16},{19,... | collective-permute-start | bytes 3096584 | tf_op jit(solution)/shard_map/ppermute | solution.py:23
  59.8 43.0 %collective-permute-start.4 = (f32[7,8,32,144]{3,2,1,0:T(8,128)S(1)}, f32[7,8,32,144]{3,2,1,0:T(8,128)S(1)}, u32[]{:S(2)}, u32[]{:S(2)}) collective-permute-start(f32[7,8,32,144]{3,2,1,0:T(8,128)S(1)} %pad_maximum_fusion.1), channel_id=1, source_target_pairs={{0,1},{2,3},{4,5},{6,7},{8,9},{10,11},{12,13},{14,15},{16,17},{18,... | collective-permute-start | bytes 3096584 | tf_op jit(solution)/shard_map/ppermute | solution.py:21
  110.5 20.0 %collective-permute-start.13 = (f32[7,8,16,8]{3,1,2,0:T(8,128)S(1)}, f32[7,8,16,8]{3,1,2,0:T(8,128)S(1)}, u32[]{:S(2)}, u32[]{:S(2)}) collective-permute-start(f32[7,8,16,8]{3,1,2,0:T(8,128)S(1)} %get-tuple-element.29), channel_id=1, source_target_pairs={{32,0},{64,32},{96,64},{128,96},{160,128},{192,160},{224,192},{256... | collective-permute-start | bytes 86024 | tf_op jit(solution)/shard_map/ppermute | solution.py:23
  112.4 26.4 %collective-permute-start.12 = (f32[7,8,16,8]{3,1,2,0:T(8,128)S(1)}, f32[7,8,16,8]{3,1,2,0:T(8,128)S(1)}, u32[]{:S(2)}, u32[]{:S(2)}) collective-permute-start(f32[7,8,16,8]{3,1,2,0:T(8,128)S(1)} %get-tuple-element.28), channel_id=1, source_target_pairs={{0,32},{32,64},{64,96},{96,128},{128,160},{160,192},{192,224},{224... | collective-permute-start | bytes 86024 | tf_op jit(solution)/shard_map/ppermute | solution.py:21
  139.3 7.9 %collective-permute-start.15 = (f32[7,8,8,144]{3,1,2,0:T(8,128)S(1)}, f32[7,8,8,144]{3,1,2,0:T(8,128)S(1)}, u32[]{:S(2)}, u32[]{:S(2)}) collective-permute-start(f32[7,8,8,144]{3,1,2,0:T(8,128)S(1)} %get-tuple-element.21), channel_id=1, source_target_pairs={{2,0},{4,2},{6,4},{8,6},{10,8},{12,10},{14,12},{16,14},{18,16},{20... | collective-permute-start | bytes 774152 | tf_op jit(solution)/shard_map/ppermute | solution.py:23
  141.2 9.8 %collective-permute-start.14 = (f32[7,8,8,144]{3,1,2,0:T(8,128)S(1)}, f32[7,8,8,144]{3,1,2,0:T(8,128)S(1)}, u32[]{:S(2)}, u32[]{:S(2)}) collective-permute-start(f32[7,8,8,144]{3,1,2,0:T(8,128)S(1)} %get-tuple-element.20), channel_id=1, source_target_pairs={{0,2},{2,4},{4,6},{6,8},{8,10},{10,12},{12,14},{14,16},{16,18},{18... | collective-permute-start | bytes 774152 | tf_op jit(solution)/shard_map/ppermute | solution.py:21
  151.4 68.6 %collective-permute-start.17 = (f32[7,8,32,144]{3,1,2,0:T(8,128)S(1)}, f32[7,8,32,144]{3,1,2,0:T(8,128)S(1)}, u32[]{:S(2)}, u32[]{:S(2)}) collective-permute-start(f32[7,8,32,144]{3,1,2,0:T(8,128)S(1)} %pad_maximum_fusion.2), channel_id=1, source_target_pairs={{1,0},{3,2},{5,4},{7,6},{9,8},{11,10},{13,12},{15,14},{17,16},{19,... | collective-permute-start | bytes 3096584 | tf_op jit(solution)/shard_map/ppermute | solution.py:23
  152.7 67.3 %collective-permute-start.16 = (f32[7,8,32,144]{3,1,2,0:T(8,128)S(1)}, f32[7,8,32,144]{3,1,2,0:T(8,128)S(1)}, u32[]{:S(2)}, u32[]{:S(2)}) collective-permute-start(f32[7,8,32,144]{3,1,2,0:T(8,128)S(1)} %pad_maximum_fusion.2), channel_id=1, source_target_pairs={{0,1},{2,3},{4,5},{6,7},{8,9},{10,11},{12,13},{14,15},{16,17},{18,... | collective-permute-start | bytes 3096584 | tf_op jit(solution)/shard_map/ppermute | solution.py:21
  157.5 5.8 %collective-permute-start.9 = (f32[4,8,1,128]{3,1,2,0:T(8,128)S(1)}, f32[4,8,1,128]{3,1,2,0:T(8,128)S(1)}, u32[]{:S(2)}, u32[]{:S(2)}) collective-permute-start(f32[4,8,1,128]{3,1,2,0:T(8,128)S(1)} %get-tuple-element.26), channel_id=1, source_target_pairs={{0,2},{2,4},{4,6},{6,8},{8,10},{10,12},{12,14},{14,16},{16,18},{18... | collective-permute-start | bytes 49160 | tf_op jit(solution)/shard_map/ppermute | solution.py:21
  160.8 5.6 %collective-permute-start.8 = (f32[4,8,1,128]{3,1,2,0:T(8,128)S(1)}, f32[4,8,1,128]{3,1,2,0:T(8,128)S(1)}, u32[]{:S(2)}, u32[]{:S(2)}) collective-permute-start(f32[4,8,1,128]{3,1,2,0:T(8,128)S(1)} %get-tuple-element.27), channel_id=1, source_target_pairs={{2,0},{4,2},{6,4},{8,6},{10,8},{12,10},{14,12},{16,14},{18,16},{20... | collective-permute-start | bytes 49160 | tf_op jit(solution)/shard_map/ppermute | solution.py:23
  166.5 53.2 %collective-permute-start.11 = (f32[4,1,18,128]{3,1,2,0:T(1,128)S(1)}, f32[4,1,18,128]{3,1,2,0:T(1,128)S(1)}, u32[]{:S(2)}, u32[]{:S(2)}) collective-permute-start(f32[4,1,18,128]{3,1,2,0:T(1,128)S(1)} %get-tuple-element.35), channel_id=1, source_target_pairs={{0,1},{2,3},{4,5},{6,7},{8,9},{10,11},{12,13},{14,15},{16,17},{18,... | collective-permute-start | bytes 110600 | tf_op jit(solution)/shard_map/ppermute | solution.py:21
  167.8 51.9 %collective-permute-start.10 = (f32[4,1,18,128]{3,1,2,0:T(1,128)S(1)}, f32[4,1,18,128]{3,1,2,0:T(1,128)S(1)}, u32[]{:S(2)}, u32[]{:S(2)}) collective-permute-start(f32[4,1,18,128]{3,1,2,0:T(1,128)S(1)} %get-tuple-element.34), channel_id=1, source_target_pairs={{1,0},{3,2},{5,4},{7,6},{9,8},{11,10},{13,12},{15,14},{17,16},{19,... | collective-permute-start | bytes 110600 | tf_op jit(solution)/shard_map/ppermute | solution.py:23
  169.2 40.1 %collective-permute-start.7 = (f32[4,8,16,1]{3,1,2,0:T(8,128)S(1)}, f32[4,8,16,1]{3,1,2,0:T(8,128)S(1)}, u32[]{:S(2)}, u32[]{:S(2)}) collective-permute-start(f32[4,8,16,1]{3,1,2,0:T(8,128)S(1)} %get-tuple-element.25), channel_id=1, source_target_pairs={{0,32},{32,64},{64,96},{96,128},{128,160},{160,192},{192,224},{224... | collective-permute-start | bytes 6152 | tf_op jit(solution)/shard_map/ppermute | solution.py:21
  209.3 10.3 %collective-permute-start.6 = (f32[4,8,16,1]{3,1,2,0:T(8,128)S(1)}, f32[4,8,16,1]{3,1,2,0:T(8,128)S(1)}, u32[]{:S(2)}, u32[]{:S(2)}) collective-permute-start(f32[4,8,16,1]{3,1,2,0:T(8,128)S(1)} %get-tuple-element.24), channel_id=1, source_target_pairs={{32,0},{64,32},{96,64},{128,96},{160,128},{192,160},{224,192},{256... | collective-permute-start | bytes 6152 | tf_op jit(solution)/shard_map/ppermute | solution.py:23
where the time goes:
time: 372 us
  waiting for transfers between devices  151 us (41%)
  blocking collectives  138 us (37%)
  starting transfers between devices  53.8 us (14%)
  matrix products  15.9 us (4%)
  other arithmetic  9.48 us (3%)
    psum x1, blocking collectives, shards(): lax.psum((sums[0], sums[1], sums[2], sums[3], sums[4]), ('span', 'stream'))  138 us
    ppermute x9, waiting for transfers between devices, with_halo(): lax.ppermute(head, axis, [((i + 1) % count, i) for i in range(ends)])  87.4 us
    ppermute x9, waiting for transfers between devices, with_halo(): lax.ppermute(tail, axis, [(i, (i + 1) % count) for i in range(ends)])  63.8 us
    ppermute x9, starting transfers between devices, with_halo(): lax.ppermute(head, axis, [((i + 1) % count, i) for i in range(ends)])  27.1 us
    ppermute x9, starting transfers between devices, with_halo(): lax.ppermute(tail, axis, [(i, (i + 1) % count) for i in range(ends)])  26.7 us
    dot_general x2, matrix products, smooth(): jnp.einsum('fswz,zk->fswk', padded, matrix, precision=lax.Precision.HIGHEST)  10.5 us
  transfers between devices with their start and end apart: 18, of which 13 were waited for; matrix products, arithmetic and copies ran while one was open for 0% of the time, Pallas kernels for 0%

commit v1 on v0

--- a/solution.py
+++ b/solution.py
@@ -8,6 +8,11 @@
 filter_taps = [value / sum(raw_taps) for value in raw_taps]
 clark_coef = 9.0
 small_eps = 1e-06
+
+
+def start_sheet(x0):
+    tmp = lax.psum(lax.psum(x0, "span"), "stream")
+    return tmp
 
 
 def with_halo(cells, sides, width, closed):
@@ -87,8 +92,8 @@
         jnp.sum(clark * clark, axis=(1, 3)),
         jnp.sum(similar * similar, axis=(1, 3)),
     )
-    cross_c, cross_s, power_e, power_c, power_s = lax.psum(
-        (sums[0], sums[1], sums[2], sums[3], sums[4]), ("span", "stream")
+    cross_c, cross_s, power_e, power_c, power_s = start_sheet(
+        (sums[0], sums[1], sums[2], sums[3], sums[4])
     )
     plane_cells = float(
         fields.shape[1] * fields.shape[3] * lax.axis_size("stream") * lax.axis_size("span")

time: 372 us -> 323 us (0.87)
  blocking collectives: 138 us -> 87.9 us
    psum x1 -> x2, blocking collectives: 138 us -> 87.9 us  [start_sheet(): tmp = lax.psum(lax.psum(x0, 'span'), 'stream')]
where the time goes in v1:
time: 323 us; the launch traced here: 322 us
  waiting for transfers between devices  151 us (47%)
  blocking collectives  87.9 us (27%)
  starting transfers between devices  53.8 us (17%)
  matrix products  15.9 us (5%)
  other arithmetic  9.49 us (3%)
    psum x2, blocking collectives, start_sheet(): tmp = lax.psum(lax.psum(x0, 'span'), 'stream')  87.9 us
    ppermute x9, waiting for transfers between devices, with_halo(): lax.ppermute(head, axis, [((i + 1) % count, i) for i in range(ends)])  87.4 us
    ppermute x9, waiting for transfers between devices, with_halo(): lax.ppermute(tail, axis, [(i, (i + 1) % count) for i in range(ends)])  63.8 us
    ppermute x9, starting transfers between devices, with_halo(): lax.ppermute(head, axis, [((i + 1) % count, i) for i in range(ends)])  27.1 us
    ppermute x9, starting transfers between devices, with_halo(): lax.ppermute(tail, axis, [(i, (i + 1) % count) for i in range(ends)])  26.7 us
    dot_general x2, matrix products, smooth(): jnp.einsum('fswz,zk->fswk', padded, matrix, precision=lax.Precision.HIGHEST)  10.5 us
  transfers between devices with their start and end apart: 18, of which 13 were waited for; matrix products, arithmetic and copies ran while one was open for 0% of the time, Pallas kernels for 0%

profile of v1, /device:TPU:16, one launch (start us, length us, event | category | flops | bytes accessed | tf_op | source)
XLA Modules:
  0.0 322.0 jit_solution(12657176683517413170)
XLA Ops:
  3.7 13.1 %collective-permute-start.1 = (f32[7,8,16,8]{3,2,1,0:T(8,128)S(1)}, f32[7,8,16,8]{3,2,1,0:T(8,128)S(1)}, u32[]{:S(2)}, u32[]{:S(2)}) collective-permute-start(f32[7,8,16,8]{3,2,1,0:T(8,128)S(1)} %get-tuple-element.36), channel_id=1, source_target_pairs={{32,0},{64,32},{96,64},{128,96},{160,128},{192,160},{224,192},{256... | collective-permute-start | bytes 86024 | tf_op jit(solution)/shard_map/ppermute | solution.py:28
  18.8 17.7 %collective-permute-done.1 = f32[7,8,16,8]{3,2,1,0:T(8,128)S(1)} collective-permute-done((f32[7,8,16,8]{3,2,1,0:T(8,128)S(1)}, f32[7,8,16,8]{3,2,1,0:T(8,128)S(1)}, u32[]{:S(2)}, u32[]{:S(2)}) %collective-permute-start.1) | collective-permute-done | bytes 28704 | tf_op jit(solution)/shard_map/ppermute | solution.py:28
  36.4 8.3 %collective-permute-done = f32[7,8,16,8]{3,2,1,0:T(8,128)S(1)} collective-permute-done((f32[7,8,16,8]{3,2,1,0:T(8,128)S(1)}, f32[7,8,16,8]{3,2,1,0:T(8,128)S(1)}, u32[]{:S(2)}, u32[]{:S(2)}) %collective-permute-start) | collective-permute-done | bytes 28704 | tf_op jit(solution)/shard_map/ppermute | solution.py:26
  48.2 2.4 collective-permute-start.2
  50.6 3.6 %collective-permute-done.3 = f32[7,8,8,144]{3,2,1,0:T(8,128)S(1)} collective-permute-done((f32[7,8,8,144]{3,2,1,0:T(8,128)S(1)}, f32[7,8,8,144]{3,2,1,0:T(8,128)S(1)}, u32[]{:S(2)}, u32[]{:S(2)}) %collective-permute-start.3) | collective-permute-done | bytes 258080 | tf_op jit(solution)/shard_map/ppermute | solution.py:28
  54.2 3.8 %collective-permute-done.2 = f32[7,8,8,144]{3,2,1,0:T(8,128)S(1)} collective-permute-done((f32[7,8,8,144]{3,2,1,0:T(8,128)S(1)}, f32[7,8,8,144]{3,2,1,0:T(8,128)S(1)}, u32[]{:S(2)}, u32[]{:S(2)}) %collective-permute-start.2) | collective-permute-done | bytes 258080 | tf_op jit(solution)/shard_map/ppermute | solution.py:26
  59.8 4.8 %collective-permute-start.4 = (f32[7,8,32,144]{3,2,1,0:T(8,128)S(1)}, f32[7,8,32,144]{3,2,1,0:T(8,128)S(1)}, u32[]{:S(2)}, u32[]{:S(2)}) collective-permute-start(f32[7,8,32,144]{3,2,1,0:T(8,128)S(1)} %pad_maximum_fusion.1), channel_id=1, source_target_pairs={{0,1},{2,3},{4,5},{6,7},{8,9},{10,11},{12,13},{14,15},{16,17},{18,... | collective-permute-start | bytes 3096584 | tf_op jit(solution)/shard_map/ppermute | solution.py:26
  64.5 36.9 %collective-permute-done.5 = f32[7,8,32,144]{3,2,1,0:T(8,128)S(1)} collective-permute-done((f32[7,8,32,144]{3,2,1,0:T(8,128)S(1)}, f32[7,8,32,144]{3,2,1,0:T(8,128)S(1)}, u32[]{:S(2)}, u32[]{:S(2)}) %collective-permute-start.5) | collective-permute-done | bytes 1032224 | tf_op jit(solution)/shard_map/ppermute | solution.py:28
  102.8 4.7 %fusion = f32[7,24,32,128]{3,2,1,0:T(8,128)S(1)} fusion(f32[7,8,32,144]{3,2,1,0:T(8,128)S(1)} %collective-permute-done.5, f32[7,8,8,144]{3,2,1,0:T(8,128)S(1)} %collective-permute-done.3, f32[7,8,16,8]{3,2,1,0:T(8,128)S(1)} %collective-permute-done.1, f32[3,8,16,128]{3,2,1,0:T(8,128)S(1)} %slice_multiply_fusion.5, f32[4,8,16,128]{3,2,1,0:T(8,128)S(1)} %copy-done, ...), kind=kOutput, calls=%fused_computation | convolution fusion | flops 1195444224 | bytes 5849088 | tf_op jit(solution)/shard_map/fswz,zk->fswk/dot_general | solution.py:49
  112.4 3.9 %collective-permute-start.12 = (f32[7,8,16,8]{3,1,2,0:T(8,128)S(1)}, f32[7,8,16,8]{3,1,2,0:T(8,128)S(1)}, u32[]{:S(2)}, u32[]{:S(2)}) collective-permute-start(f32[7,8,16,8]{3,1,2,0:T(8,128)S(1)} %get-tuple-element.33), channel_id=1, source_target_pairs={{0,32},{32,64},{64,96},{96,128},{128,160},{160,192},{192,224},{224... | collective-permute-start | bytes 86024 | tf_op jit(solution)/shard_map/ppermute | solution.py:26
  116.3 14.1 %collective-permute-done.13 = f32[7,8,16,8]{3,1,2,0:T(8,128)S(1)} collective-permute-done((f32[7,8,16,8]{3,1,2,0:T(8,128)S(1)}, f32[7,8,16,8]{3,1,2,0:T(8,128)S(1)}, u32[]{:S(2)}, u32[]{:S(2)}) %collective-permute-start.13) | collective-permute-done | bytes 28704 | tf_op jit(solution)/shard_map/ppermute | solution.py:28
  130.4 8.3 %collective-permute-done.12 = f32[7,8,16,8]{3,1,2,0:T(8,128)S(1)} collective-permute-done((f32[7,8,16,8]{3,1,2,0:T(8,128)S(1)}, f32[7,8,16,8]{3,1,2,0:T(8,128)S(1)}, u32[]{:S(2)}, u32[]{:S(2)}) %collective-permute-start.12) | collective-permute-done | bytes 28704 | tf_op jit(solution)/shard_map/ppermute | solution.py:26
  143.6 3.6 %collective-permute-done.15 = f32[7,8,8,144]{3,1,2,0:T(8,128)S(1)} collective-permute-done((f32[7,8,8,144]{3,1,2,0:T(8,128)S(1)}, f32[7,8,8,144]{3,1,2,0:T(8,128)S(1)}, u32[]{:S(2)}, u32[]{:S(2)}) %collective-permute-start.15) | collective-permute-done | bytes 258080 | tf_op jit(solution)/shard_map/ppermute | solution.py:28
  147.2 3.8 %collective-permute-done.14 = f32[7,8,8,144]{3,1,2,0:T(8,128)S(1)} collective-permute-done((f32[7,8,8,144]{3,1,2,0:T(8,128)S(1)}, f32[7,8,8,144]{3,1,2,0:T(8,128)S(1)}, u32[]{:S(2)}, u32[]{:S(2)}) %collective-permute-start.14) | collective-permute-done | bytes 258080 | tf_op jit(solution)/shard_map/ppermute | solution.py:26
  152.7 4.8 %collective-permute-start.16 = (f32[7,8,32,144]{3,1,2,0:T(8,128)S(1)}, f32[7,8,32,144]{3,1,2,0:T(8,128)S(1)}, u32[]{:S(2)}, u32[]{:S(2)}) collective-permute-start(f32[7,8,32,144]{3,1,2,0:T(8,128)S(1)} %pad_maximum_fusion.2), channel_id=1, source_target_pairs={{0,1},{2,3},{4,5},{6,7},{8,9},{10,11},{12,13},{14,15},{16,17},{18,... | collective-permute-start | bytes 3096584 | tf_op jit(solution)/shard_map/ppermute | solution.py:26
  157.5 3.3 %collective-permute-start.9 = (f32[4,8,1,128]{3,1,2,0:T(8,128)S(1)}, f32[4,8,1,128]{3,1,2,0:T(8,128)S(1)}, u32[]{:S(2)}, u32[]{:S(2)}) collective-permute-start(f32[4,8,1,128]{3,1,2,0:T(8,128)S(1)} %get-tuple-element.31), channel_id=1, source_target_pairs={{0,2},{2,4},{4,6},{6,8},{8,10},{10,12},{12,14},{14,16},{16,18},{18... | collective-permute-start | bytes 49160 | tf_op jit(solution)/shard_map/ppermute | solution.py:26
  160.8 2.5 collective-permute-start.8
  163.3 3.1 collective-permute-done.8
  171.2 38.2 %collective-permute-done.7 = f32[4,8,16,1]{3,1,2,0:T(8,128)S(1)} collective-permute-done((f32[4,8,16,1]{3,1,2,0:T(8,128)S(1)}, f32[4,8,16,1]{3,1,2,0:T(8,128)S(1)}, u32[]{:S(2)}, u32[]{:S(2)}) %collective-permute-start.7) | collective-permute-done | bytes 2080 | tf_op jit(solution)/shard_map/ppermute | solution.py:26
  211.2 8.4 %collective-permute-done.6 = f32[4,8,16,1]{3,1,2,0:T(8,128)S(1)} collective-permute-done((f32[4,8,16,1]{3,1,2,0:T(8,128)S(1)}, f32[4,8,16,1]{3,1,2,0:T(8,128)S(1)}, u32[]{:S(2)}, u32[]{:S(2)}) %collective-permute-start.6) | collective-permute-done | bytes 2080 | tf_op jit(solution)/shard_map/ppermute | solution.py:28
  220.1 2.6 pad_maximum_fusion
  222.7 5.8 %fusion.16 = f32[7,24,32,128]{3,2,1,0:T(8,128)S(1)} fusion(f32[7,24,32,144]{3,1,2,0:T(8,128)S(1)} %pad_maximum_fusion), kind=kOutput, calls=%fused_computation.17 | convolution fusion | flops 1190025216 | bytes 5849088 | tf_op jit(solution)/shard_map/fswz,zk->fswk/dot_general | solution.py:49
  231.8 81.2 %all-reduce = (f32[3,16]{1,0:T(4,128)S(1)}, f32[3,16]{1,0:T(4,128)S(1)}, f32[3,16]{1,0:T(4,128)S(1)}, f32[3,16]{1,0:T(4,128)S(1)}, f32[3,16]{1,0:T(4,128)S(1)}) all-reduce(f32[3,16]{1,0:T(4,128)S(1)} %get-tuple-element.11, f32[3,16]{1,0:T(4,128)S(1)} %get-tuple-element.12, ...), channel_id=1, replica_groups=mesh['span'=16,'wall'=16,'stream'=2] {'span'}, use_global_device_ids=true, to_apply=%region_1.2 | all-reduce | flops 240 | bytes 1920 | tf_op jit(solution)/shard_map/psum | solution.py:14
  313.0 6.7 %all-reduce.1 = (f32[3,16]{1,0:T(4,128)S(1)}, f32[3,16]{1,0:T(4,128)S(1)}, f32[3,16]{1,0:T(4,128)S(1)}, f32[3,16]{1,0:T(4,128)S(1)}, f32[3,16]{1,0:T(4,128)S(1)}) all-reduce(f32[3,16]{1,0:T(4,128)S(1)} %get-tuple-element.13, f32[3,16]{1,0:T(4,128)S(1)} %get-tuple-element.14, ...), channel_id=1, replica_groups=mesh['span'=16,'wall'=16,'stream'=2] {'stream'}, use_global_device_ids=true, to_apply=%region_2.3 | all-reduce | flops 240 | bytes 1920 | tf_op jit(solution)/shard_map/psum | solution.py:14
  (49 shorter events, 35.3 us)
Async XLA Ops:
  2.4 55.6 %copy-start = (f32[4,8,16,128]{3,2,1,0:T(8,128)S(1)}, f32[4,8,16,128]{3,2,1,0:T(8,128)}, u32[]{:S(2)}) copy-start(f32[4,8,16,128]{3,2,1,0:T(8,128)} %param.1) | copy-start | bytes 786436
  3.7 32.7 %collective-permute-start.1 = (f32[7,8,16,8]{3,2,1,0:T(8,128)S(1)}, f32[7,8,16,8]{3,2,1,0:T(8,128)S(1)}, u32[]{:S(2)}, u32[]{:S(2)}) collective-permute-start(f32[7,8,16,8]{3,2,1,0:T(8,128)S(1)} %get-tuple-element.36), channel_id=1, source_target_pairs={{32,0},{64,32},{96,64},{128,96},{160,128},{192,160},{224,192},{256... | collective-permute-start | bytes 86024 | tf_op jit(solution)/shard_map/ppermute | solution.py:28
  16.9 27.9 %collective-permute-start = (f32[7,8,16,8]{3,2,1,0:T(8,128)S(1)}, f32[7,8,16,8]{3,2,1,0:T(8,128)S(1)}, u32[]{:S(2)}, u32[]{:S(2)}) collective-permute-start(f32[7,8,16,8]{3,2,1,0:T(8,128)S(1)} %get-tuple-element.35), channel_id=1, source_target_pairs={{0,32},{32,64},{64,96},{96,128},{128,160},{160,192},{192,224},{224... | collective-permute-start | bytes 86024 | tf_op jit(solution)/shard_map/ppermute | solution.py:26
  46.3 7.9 %collective-permute-start.3 = (f32[7,8,8,144]{3,2,1,0:T(8,128)S(1)}, f32[7,8,8,144]{3,2,1,0:T(8,128)S(1)}, u32[]{:S(2)}, u32[]{:S(2)}) collective-permute-start(f32[7,8,8,144]{3,2,1,0:T(8,128)S(1)} %get-tuple-element.28), channel_id=1, source_target_pairs={{2,0},{4,2},{6,4},{8,6},{10,8},{12,10},{14,12},{16,14},{18,16},{20... | collective-permute-start | bytes 774152 | tf_op jit(solution)/shard_map/ppermute | solution.py:28
  48.2 9.8 %collective-permute-start.2 = (f32[7,8,8,144]{3,2,1,0:T(8,128)S(1)}, f32[7,8,8,144]{3,2,1,0:T(8,128)S(1)}, u32[]{:S(2)}, u32[]{:S(2)}) collective-permute-start(f32[7,8,8,144]{3,2,1,0:T(8,128)S(1)} %get-tuple-element.27), channel_id=1, source_target_pairs={{0,2},{2,4},{4,6},{6,8},{8,10},{10,12},{12,14},{14,16},{16,18},{18... | collective-permute-start | bytes 774152 | tf_op jit(solution)/shard_map/ppermute | solution.py:26
  58.5 43.0 %collective-permute-start.5 = (f32[7,8,32,144]{3,2,1,0:T(8,128)S(1)}, f32[7,8,32,144]{3,2,1,0:T(8,128)S(1)}, u32[]{:S(2)}, u32[]{:S(2)}) collective-permute-start(f32[7,8,32,144]{3,2,1,0:T(8,128)S(1)} %pad_maximum_fusion.1), channel_id=1, source_target_pairs={{1,0},{3,2},{5,4},{7,6},{9,8},{11,10},{13,12},{15,14},{17,16},{19,... | collective-permute-start | bytes 3096584 | tf_op jit(solution)/shard_map/ppermute | solution.py:28
  59.8 43.0 %collective-permute-start.4 = (f32[7,8,32,144]{3,2,1,0:T(8,128)S(1)}, f32[7,8,32,144]{3,2,1,0:T(8,128)S(1)}, u32[]{:S(2)}, u32[]{:S(2)}) collective-permute-start(f32[7,8,32,144]{3,2,1,0:T(8,128)S(1)} %pad_maximum_fusion.1), channel_id=1, source_target_pairs={{0,1},{2,3},{4,5},{6,7},{8,9},{10,11},{12,13},{14,15},{16,17},{18,... | collective-permute-start | bytes 3096584 | tf_op jit(solution)/shard_map/ppermute | solution.py:26
  110.5 20.0 %collective-permute-start.13 = (f32[7,8,16,8]{3,1,2,0:T(8,128)S(1)}, f32[7,8,16,8]{3,1,2,0:T(8,128)S(1)}, u32[]{:S(2)}, u32[]{:S(2)}) collective-permute-start(f32[7,8,16,8]{3,1,2,0:T(8,128)S(1)} %get-tuple-element.34), channel_id=1, source_target_pairs={{32,0},{64,32},{96,64},{128,96},{160,128},{192,160},{224,192},{256... | collective-permute-start | bytes 86024 | tf_op jit(solution)/shard_map/ppermute | solution.py:28
  112.4 26.4 %collective-permute-start.12 = (f32[7,8,16,8]{3,1,2,0:T(8,128)S(1)}, f32[7,8,16,8]{3,1,2,0:T(8,128)S(1)}, u32[]{:S(2)}, u32[]{:S(2)}) collective-permute-start(f32[7,8,16,8]{3,1,2,0:T(8,128)S(1)} %get-tuple-element.33), channel_id=1, source_target_pairs={{0,32},{32,64},{64,96},{96,128},{128,160},{160,192},{192,224},{224... | collective-permute-start | bytes 86024 | tf_op jit(solution)/shard_map/ppermute | solution.py:26
  139.3 7.9 %collective-permute-start.15 = (f32[7,8,8,144]{3,1,2,0:T(8,128)S(1)}, f32[7,8,8,144]{3,1,2,0:T(8,128)S(1)}, u32[]{:S(2)}, u32[]{:S(2)}) collective-permute-start(f32[7,8,8,144]{3,1,2,0:T(8,128)S(1)} %get-tuple-element.26), channel_id=1, source_target_pairs={{2,0},{4,2},{6,4},{8,6},{10,8},{12,10},{14,12},{16,14},{18,16},{20... | collective-permute-start | bytes 774152 | tf_op jit(solution)/shard_map/ppermute | solution.py:28
  141.2 9.8 %collective-permute-start.14 = (f32[7,8,8,144]{3,1,2,0:T(8,128)S(1)}, f32[7,8,8,144]{3,1,2,0:T(8,128)S(1)}, u32[]{:S(2)}, u32[]{:S(2)}) collective-permute-start(f32[7,8,8,144]{3,1,2,0:T(8,128)S(1)} %get-tuple-element.25), channel_id=1, source_target_pairs={{0,2},{2,4},{4,6},{6,8},{8,10},{10,12},{12,14},{14,16},{16,18},{18... | collective-permute-start | bytes 774152 | tf_op jit(solution)/shard_map/ppermute | solution.py:26
  151.4 68.6 %collective-permute-start.17 = (f32[7,8,32,144]{3,1,2,0:T(8,128)S(1)}, f32[7,8,32,144]{3,1,2,0:T(8,128)S(1)}, u32[]{:S(2)}, u32[]{:S(2)}) collective-permute-start(f32[7,8,32,144]{3,1,2,0:T(8,128)S(1)} %pad_maximum_fusion.2), channel_id=1, source_target_pairs={{1,0},{3,2},{5,4},{7,6},{9,8},{11,10},{13,12},{15,14},{17,16},{19,... | collective-permute-start | bytes 3096584 | tf_op jit(solution)/shard_map/ppermute | solution.py:28
  152.7 67.3 %collective-permute-start.16 = (f32[7,8,32,144]{3,1,2,0:T(8,128)S(1)}, f32[7,8,32,144]{3,1,2,0:T(8,128)S(1)}, u32[]{:S(2)}, u32[]{:S(2)}) collective-permute-start(f32[7,8,32,144]{3,1,2,0:T(8,128)S(1)} %pad_maximum_fusion.2), channel_id=1, source_target_pairs={{0,1},{2,3},{4,5},{6,7},{8,9},{10,11},{12,13},{14,15},{16,17},{18,... | collective-permute-start | bytes 3096584 | tf_op jit(solution)/shard_map/ppermute | solution.py:26
  157.5 5.8 %collective-permute-start.9 = (f32[4,8,1,128]{3,1,2,0:T(8,128)S(1)}, f32[4,8,1,128]{3,1,2,0:T(8,128)S(1)}, u32[]{:S(2)}, u32[]{:S(2)}) collective-permute-start(f32[4,8,1,128]{3,1,2,0:T(8,128)S(1)} %get-tuple-element.31), channel_id=1, source_target_pairs={{0,2},{2,4},{4,6},{6,8},{8,10},{10,12},{12,14},{14,16},{16,18},{18... | collective-permute-start | bytes 49160 | tf_op jit(solution)/shard_map/ppermute | solution.py:26
  160.8 5.6 %collective-permute-start.8 = (f32[4,8,1,128]{3,1,2,0:T(8,128)S(1)}, f32[4,8,1,128]{3,1,2,0:T(8,128)S(1)}, u32[]{:S(2)}, u32[]{:S(2)}) collective-permute-start(f32[4,8,1,128]{3,1,2,0:T(8,128)S(1)} %get-tuple-element.32), channel_id=1, source_target_pairs={{2,0},{4,2},{6,4},{8,6},{10,8},{12,10},{14,12},{16,14},{18,16},{20... | collective-permute-start | bytes 49160 | tf_op jit(solution)/shard_map/ppermute | solution.py:28
  166.5 53.2 %collective-permute-start.11 = (f32[4,1,18,128]{3,1,2,0:T(1,128)S(1)}, f32[4,1,18,128]{3,1,2,0:T(1,128)S(1)}, u32[]{:S(2)}, u32[]{:S(2)}) collective-permute-start(f32[4,1,18,128]{3,1,2,0:T(1,128)S(1)} %get-tuple-element.40), channel_id=1, source_target_pairs={{0,1},{2,3},{4,5},{6,7},{8,9},{10,11},{12,13},{14,15},{16,17},{18,... | collective-permute-start | bytes 110600 | tf_op jit(solution)/shard_map/ppermute | solution.py:26
  167.8 51.9 %collective-permute-start.10 = (f32[4,1,18,128]{3,1,2,0:T(1,128)S(1)}, f32[4,1,18,128]{3,1,2,0:T(1,128)S(1)}, u32[]{:S(2)}, u32[]{:S(2)}) collective-permute-start(f32[4,1,18,128]{3,1,2,0:T(1,128)S(1)} %get-tuple-element.39), channel_id=1, source_target_pairs={{1,0},{3,2},{5,4},{7,6},{9,8},{11,10},{13,12},{15,14},{17,16},{19,... | collective-permute-start | bytes 110600 | tf_op jit(solution)/shard_map/ppermute | solution.py:28
  169.2 40.1 %collective-permute-start.7 = (f32[4,8,16,1]{3,1,2,0:T(8,128)S(1)}, f32[4,8,16,1]{3,1,2,0:T(8,128)S(1)}, u32[]{:S(2)}, u32[]{:S(2)}) collective-permute-start(f32[4,8,16,1]{3,1,2,0:T(8,128)S(1)} %get-tuple-element.30), channel_id=1, source_target_pairs={{0,32},{32,64},{64,96},{96,128},{128,160},{160,192},{192,224},{224... | collective-permute-start | bytes 6152 | tf_op jit(solution)/shard_map/ppermute | solution.py:26
  209.3 10.3 %collective-permute-start.6 = (f32[4,8,16,1]{3,1,2,0:T(8,128)S(1)}, f32[4,8,16,1]{3,1,2,0:T(8,128)S(1)}, u32[]{:S(2)}, u32[]{:S(2)}) collective-permute-start(f32[4,8,16,1]{3,1,2,0:T(8,128)S(1)} %get-tuple-element.29), channel_id=1, source_target_pairs={{32,0},{64,32},{96,64},{128,96},{160,128},{192,160},{224,192},{256... | collective-permute-start | bytes 6152 | tf_op jit(solution)/shard_map/ppermute | solution.py:28
